TPU v7x, 256 devices: a whole 4x4x8 slice. The times are simulated.
256 devices in a mesh: wave: 64 (over z, y, core), field: 4 (over x).
Axes of the slice: x: 4, y: 4, z: 8, core: 2. Of those that a mesh axis runs over, the one named last changes fastest.
Arguments:
- spectra: bfloat16 [640, 2, 160, 640], P('wave', None, 'field'), may hold values from -0.15625 to 0.15625
- legendre: bfloat16 [640, 640, 640], P('wave'), may hold values from -0.25 to 0.25
- block_mask: int32 [640, 10, 10], P('wave'), may hold values from 0 to 1, as said below
- wave_slot: int32 [640], replicated, may hold values from 0 to 639, as said below
- lat_order: int32 [1280], replicated, may hold values from 0 to 1279, each once
- level_order: int32 [160], replicated, may hold values from 0 to 159, each once
Outputs:
- grid_fields: bfloat16 [1280, 160, 3072], P('wave', None, 'field')
Inputs may be any that keep to these rules, and one draw needn't show every extreme that they name: `wave_slot`: each wavenumber from 0 to 639 is held by exactly one slot. `block_mask`: a block is 0 where every total wavenumber of its row block lies below the slot's wavenumber; otherwise it is 0 only in the first few latitude blocks from the pole, fewer than half of them.
All inputs are finite; a program needn't handle non-finite values.
Results may differ from a plain program's by a relative error of at most 0.009.
Values may be sent and summed in bfloat16 or wider, within the bound.
A program may use at most 128 MiB of HBM per device.

v0:
```python
import math
import jax
import jax.numpy as jnp
from jax import lax
from jax.sharding import PartitionSpec as P

BLOCK = 64
NLON = 3072


def spread_mask(block_mask):
    grown = jnp.repeat(jnp.repeat(block_mask, BLOCK, axis=1), BLOCK, axis=2)
    return grown > 0


def fourier_tables(wave_slot, lon_index):
    wavenums = jnp.repeat(wave_slot, 2)
    component = jnp.arange(wavenums.shape[0], dtype=jnp.int32) % 2
    phases = wavenums[:, None] * lon_index[None, :] % NLON
    angles = phases.astype(jnp.float32) * jnp.float32(2.0 * math.pi / NLON)
    weight = jnp.where(wavenums == 0, jnp.float32(1.0), jnp.float32(2.0))[:, None]
    entries = jnp.where(
        component[:, None] == 0, weight * jnp.cos(angles), -weight * jnp.sin(angles)
    )
    high_part = entries.astype(jnp.bfloat16)
    low_part = (entries - high_part.astype(jnp.float32)).astype(jnp.bfloat16)
    slots = wave_slot.shape[0]
    return (
        high_part.reshape(slots, 2, lon_index.shape[0]),
        low_part.reshape(slots, 2, lon_index.shape[0]),
    )


def synthesize(coeff_rows, high_part, low_part):
    from_high = jnp.einsum(
        "stcl,scq->tlq", coeff_rows, high_part, preferred_element_type=jnp.float32
    )
    from_low = jnp.einsum("stcl,scq->tlq", coeff_rows, low_part, preferred_element_type=jnp.float32)
    return (from_high + from_low).astype(jnp.bfloat16)


def shards(spectra, legendre, block_mask, wave_slot, lat_order, level_order):
    slot_count = spectra.shape[0]
    spec_len = spectra.shape[3]
    first_slot = lax.axis_index("wave") * slot_count
    my_waves = lax.dynamic_slice_in_dim(wave_slot, first_slot, slot_count)
    degree = jnp.arange(spec_len, dtype=jnp.int32)
    upper_tri = degree[None, :] >= my_waves[:, None]
    even_deg = (degree[None, :] + my_waves[:, None]) % 2 == 0
    zero_bf = jnp.zeros((), jnp.bfloat16)
    even_spec = jnp.where((upper_tri & even_deg)[:, None, None, :], spectra, zero_bf)
    odd_spec = jnp.where((upper_tri & ~even_deg)[:, None, None, :], spectra, zero_bf)
    kept_poly = jnp.where(spread_mask(block_mask), legendre, zero_bf)
    even_sum = jnp.einsum(
        "snj,scln->sjcl", kept_poly, even_spec, preferred_element_type=jnp.float32
    )
    odd_sum = jnp.einsum("snj,scln->sjcl", kept_poly, odd_spec, preferred_element_type=jnp.float32)
    northern = even_sum + odd_sum
    southern = (even_sum - odd_sum)[:, ::-1]
    coeffs = jnp.concatenate([northern, southern], axis=1).astype(jnp.bfloat16)
    coeffs = jnp.take(coeffs, lat_order, axis=1)
    by_latitude = lax.all_to_all(coeffs, "wave", split_axis=1, concat_axis=0, tiled=True)
    high_part, low_part = fourier_tables(wave_slot, jnp.arange(NLON, dtype=jnp.int32))
    grid_local = synthesize(by_latitude, high_part, low_part)
    columns = lax.all_to_all(grid_local, "field", split_axis=2, concat_axis=1, tiled=True)
    return jnp.take(columns, level_order, axis=1)


def solution(mesh):
    placed = (
        P("wave", None, "field", None),
        P("wave", None, None),
        P("wave", None, None),
        P(),
        P(),
        P(),
    )
    return jax.shard_map(
        shards, mesh=mesh, in_specs=placed, out_specs=P("wave", None, "field"), check_vma=False
    )
```

profile of v0, /device:TPU:1, one launch (start us, length us, event | category | flops | bytes accessed | tf_op | source)
XLA Modules:
  0.0 450.5 jit_solution(13107642925932214233)
XLA Ops:
  2.3 12.9 %copy.33 = bf16[10,640,640]{1,2,0:T(8,128)(2,1)} copy(bf16[10,640,640]{2,1,0:T(8,128)(2,1)} %param.7) | data formatting | bytes 16384000 | tf_op args[1]
  16.0 7.6 %bitcast_select_fusion = bf16[10,640,640]{1,2,0:T(8,128)(2,1)} fusion(bf16[10,640,640]{1,2,0:T(8,128)(2,1)} %copy.33, pred[10,640,10]{1,2,0:T(8,128)(4,1)S(1)} %gt.16), kind=kLoop, calls=%fused_computation.3 | loop fusion | flops 4096000 | bytes 16448000 | tf_op jit(solution)/shard_map/jit(_where)/select_n | solution.py:53
  23.6 6.5 %fusion.6 = f32[10,640,2,40]{1,3,2,0:T(8,128)S(1)} fusion(bf16[10,640,640]{1,2,0:T(8,128)(2,1)} %bitcast_select_fusion, bf16[10,2,40,640]{3,2,1,0:T(8,128)(2,1)S(1)} %copy-done.1, pred[10,640]{1,0:T(8,128)(4,1)S(1)} %get-tuple-element.7), kind=kOutput, calls=%fused_computation.15 | convolution fusion | flops 655872000 | bytes 11270400 | tf_op jit(solution)/shard_map/snj,scln->sjcl/dot_general | solution.py:57
  37.3 9.8 %copy.36 = bf16[10,1280,2,40]{3,2,1,0:T(2,128)(2,1)} copy(bf16[10,1280,2,40]{1,3,2,0:T(8,128)(2,1)S(1)} %pad_maximum_fusion) | data formatting | bytes 4096000 | tf_op jit(solution)/shard_map/concatenate | solution.py:60
  47.1 46.7 %gather_fusion = bf16[1280,10,2,40]{3,2,1,0:T(2,128)(2,1)} fusion(bf16[10,1280,2,40]{3,2,1,0:T(2,128)(2,1)} %copy.36, s32[2048]{0:T(1024)S(1)} %pad_clamp_fusion), kind=kCustom, calls=%fused_computation | custom fusion | bytes 4101120 | tf_op jit(solution)/shard_map/jit(_take)/gather | solution.py:61
  93.8 11.2 %fusion.45 = bf16[1280,10,2,40]{3,2,1,0:T(2,128)(2,1)} fusion(bf16[1280,10,2,40]{3,2,1,0:T(2,128)(2,1)} %gather_fusion, pred[1280]{0:T(1024)(128)(4,1)S(1)} %compare_and_fusion), kind=kLoop, calls=%fused_computation.65 | loop fusion | flops 1024000 | bytes 4097280
  105.0 11.3 %reshape.183 = bf16[64,2,8000]{2,1,0:T(2,128)(2,1)} reshape(bf16[1280,10,2,40]{3,2,1,0:T(2,128)(2,1)} %fusion.45) | data formatting | bytes 4096000
  116.4 13.4 %all-to-all-start = ((bf16[64,2,8000]{2,1,0:T(2,128)(2,1)}), bf16[64,2,8000]{2,1,0:T(2,128)(2,1)S(1)}, u32[]{:S(2)}, u32[]{:S(2)}) async-start(bf16[64,2,8000]{2,1,0:T(2,128)(2,1)} %reshape.183), calls=%async_computation | async-start | bytes 4128768 | tf_op jit(solution)/shard_map/all_to_all | solution.py:62
  129.9 36.1 %fusion.54 = bf16[640,2,3072,1]{2,0,1,3:T(8,128)(2,1)} fusion(f32[640]{0:T(1024)S(1)} %get-tuple-element.6, s32[640]{0:T(1024)S(1)} %copy-done.3, f32[640]{0:T(1024)S(1)} %get-tuple-element.5, pred[640,2]{0,1:T(4,128)(4,1)S(1)} %fusion.34), kind=kLoop, calls=%fused_computation.22.clone.clone.clone.1 | loop fusion | flops 51118080 | bytes 7873280 | tf_op jit(solution)/shard_map/stcl,scq->tlq/dot_general | solution.py:35
  166.0 36.7 %fusion.56 = bf16[640,2,3072,1]{2,0,1,3:T(8,128)(2,1)} fusion(f32[640]{0:T(1024)S(1)} %get-tuple-element.6, s32[640]{0:T(1024)S(1)} %copy-done.3, f32[640]{0:T(1024)S(1)} %get-tuple-element.5, pred[640,2]{0,1:T(4,128)(4,1)S(1)} %fusion.34), kind=kLoop, calls=%fused_computation.19.clone.clone.1 | loop fusion | flops 62914560 | bytes 7873280 | tf_op jit(solution)/shard_map/stcl,scq->tlq/dot_general | solution.py:38
  202.7 8.0 %reshape.184 = bf16[1280,10,2,40]{3,2,1,0:T(2,128)(2,1)} reshape(bf16[64,2,8000]{2,1,0:T(2,128)(2,1)S(1)} %all-to-all-done) | data formatting | bytes 4096000
  210.7 6.8 %copy.38 = bf16[64,10,20,2,40]{4,3,2,1,0:T(2,128)(2,1)} copy(bf16[64,10,20,2,40]{4,3,1,2,0:T(2,128)(2,1)} %bitcast.65) | data formatting | bytes 4096000 | tf_op jit(solution)/shard_map/all_to_all | solution.py:62
  217.5 11.9 %copy.39 = bf16[640,20,2,40]{0,3,2,1:T(8,128)(2,1)S(1)} copy(bf16[640,20,2,40]{3,2,1,0:T(2,128)(2,1)} %bitcast.66) | data formatting | bytes 4096000 | tf_op jit(solution)/shard_map/all_to_all | solution.py:62
  229.5 8.9 %fusion.11 = f32[20,40,3072,1]{2,1,3,0:T(8,128)S(1)} fusion(bf16[640,20,2,40]{0,3,2,1:T(8,128)(2,1)S(1)} %copy.39, bf16[640,2,3072,1]{2,0,1,3:T(8,128)(2,1)} %fusion.56), kind=kOutput, calls=%fused_computation.20 | convolution fusion | flops 6291456000 | bytes 19742720 | tf_op jit(solution)/shard_map/stcl,scq->tlq/dot_general | solution.py:38
  238.3 11.4 %fusion.5 = bf16[20,40,3072]{2,1,0:T(8,128)(2,1)} fusion(f32[20,40,3072,1]{2,1,3,0:T(8,128)S(1)} %fusion.11, bf16[640,20,2,40]{0,3,2,1:T(8,128)(2,1)S(1)} %copy.39, bf16[640,2,3072,1]{2,0,1,3:T(8,128)(2,1)} %fusion.54), kind=kOutput, calls=%fused_computation.14 | convolution fusion | flops 6296371200 | bytes 24657920 | tf_op jit(solution)/shard_map/stcl,scq->tlq/dot_general | solution.py:35
  249.8 19.3 %copy.41 = bf16[20,40,3072]{1,0,2:T(8,128)(2,1)} copy(bf16[20,40,3072]{2,1,0:T(8,128)(2,1)} %fusion.5) | data formatting | bytes 9830400 | tf_op jit(solution)/shard_map/convert_element_type | solution.py:39
  269.1 35.7 %reshape.185 = bf16[4,2,307200]{2,1,0:T(2,128)(2,1)} reshape(bf16[3072,20,40]{2,1,0:T(8,128)(2,1)} %bitcast.63) | data formatting | bytes 9830400
  304.8 5.4 %all-to-all-start.1 = ((bf16[4,2,307200]{2,1,0:T(2,128)(2,1)}), bf16[4,2,307200]{2,1,0:T(2,128)(2,1)}, u32[]{:S(2)}, u32[]{:S(2)}) async-start(bf16[4,2,307200]{2,1,0:T(2,128)(2,1)} %reshape.185), calls=%async_computation.1 | async-start | bytes 9830400 | tf_op jit(solution)/shard_map/all_to_all | solution.py:65
  310.2 56.3 %all-to-all-done.1 = bf16[4,2,307200]{2,1,0:T(2,128)(2,1)} async-done(((bf16[4,2,307200]{2,1,0:T(2,128)(2,1)}), bf16[4,2,307200]{2,1,0:T(2,128)(2,1)}, u32[]{:S(2)}, u32[]{:S(2)}) %all-to-all-start.1) | async-done | bytes 4915232 | tf_op jit(solution)/shard_map/all_to_all | solution.py:65
  366.5 36.9 %reshape.186 = bf16[3072,20,40]{2,1,0:T(8,128)(2,1)} reshape(bf16[4,2,307200]{2,1,0:T(2,128)(2,1)} %all-to-all-done.1) | data formatting | bytes 9830400
  403.4 20.9 %copy.55 = bf16[20,40,4,768]{3,2,1,0:T(4,128)(2,1)} copy(bf16[20,40,4,768]{1,0,3,2:T(8,128)(2,1)} %bitcast.64) | data formatting | bytes 9830400 | tf_op jit(solution)/shard_map/all_to_all | solution.py:65
  424.3 7.7 %copy.56 = bf16[20,4,40,768]{3,0,2,1:T(8,128)(2,1)} copy(bf16[20,4,40,768]{3,1,2,0:T(4,128)(2,1)} %bitcast.68) | data formatting | bytes 9830400 | tf_op jit(solution)/shard_map/all_to_all | solution.py:65
  432.0 11.3 %gather_fusion.1 = bf16[160,20,768]{2,1,0:T(8,128)(2,1)} fusion(bf16[20,160,768]{2,0,1:T(8,128)(2,1)} %bitcast.67, s32[1024]{0:T(1024)S(1)} %pad_clamp_fusion.1), kind=kCustom, calls=%fused_computation.1 | custom fusion | bytes 9831040 | tf_op jit(solution)/shard_map/jit(_take)/gather | solution.py:66
  446.6 3.3 copy.45
  (30 shorter events, 13.6 us)
Async XLA Ops:
  2.3 12.9 %copy-start.2 = (s32[10,10,10]{2,1,0:T(8,128)S(1)}, s32[10,10,10]{2,1,0:T(8,128)}, u32[]{:S(2)}) copy-start(s32[10,10,10]{2,1,0:T(8,128)} %param.8) | copy-start | bytes 12004
  16.0 7.6 %copy-start.1 = (bf16[10,2,40,640]{3,2,1,0:T(8,128)(2,1)S(1)}, bf16[10,2,40,640]{3,2,1,0:T(8,128)(2,1)}, u32[]{:S(2)}) copy-start(bf16[10,2,40,640]{3,2,1,0:T(8,128)(2,1)} %param.6) | copy-start | bytes 3072004
  23.6 6.5 %copy-start = (bf16[10,640,640]{1,2,0:T(8,128)(2,1)S(1)}, bf16[10,640,640]{1,2,0:T(8,128)(2,1)}, u32[]{:S(2)}) copy-start(bf16[10,640,640]{1,2,0:T(8,128)(2,1)} %bitcast_select_fusion) | copy-start | bytes 24576004
  105.0 24.8 %copy-start.3 = (s32[640]{0:T(1024)S(1)}, s32[640]{0:T(1024)}, u32[]{:S(2)}) copy-start(s32[640]{0:T(1024)} %param.9) | copy-start | bytes 7684
  116.4 86.3 %all-to-all-start = ((bf16[64,2,8000]{2,1,0:T(2,128)(2,1)}), bf16[64,2,8000]{2,1,0:T(2,128)(2,1)S(1)}, u32[]{:S(2)}, u32[]{:S(2)}) async-start(bf16[64,2,8000]{2,1,0:T(2,128)(2,1)} %reshape.183), calls=%async_computation | async-start | bytes 4128768 | tf_op jit(solution)/shard_map/all_to_all | solution.py:62
  304.8 5.4 %copy-start.4 = (s32[160]{0:T(256)S(1)}, s32[160]{0:T(256)}, u32[]{:S(2)}) copy-start(s32[160]{0:T(256)} %param.11) | copy-start | bytes 1924
  304.8 61.7 %all-to-all-start.1 = ((bf16[4,2,307200]{2,1,0:T(2,128)(2,1)}), bf16[4,2,307200]{2,1,0:T(2,128)(2,1)}, u32[]{:S(2)}, u32[]{:S(2)}) async-start(bf16[4,2,307200]{2,1,0:T(2,128)(2,1)} %reshape.185), calls=%async_computation.1 | async-start | bytes 9830400 | tf_op jit(solution)/shard_map/all_to_all | solution.py:65
where the time goes:
time: 458 us; the launch traced here: 450 us
  local copies, waits for them, and re-layouts  247 us (54%)
  other arithmetic  98.1 us (21%)
  waiting for transfers between devices  56.3 us (12%)
  matrix products  29.8 us (7%)
  starting transfers between devices  18.8 us (4%)
    unnamed x15, local copies, waits for them, and re-layouts  105 us
    all_to_all x1, waiting for transfers between devices, shards(): lax.all_to_all(grid_local, 'field', split_axis=2, concat_axis=1, tiled=True)  56.3 us
    gather x1, local copies, waits for them, and re-layouts, shards(): coeffs = jnp.take(coeffs, lat_order, axis=1)  46.7 us
    dot_general x1, other arithmetic, synthesize(): jnp.einsum('stcl,scq->tlq', coeff_rows, low_part, preferred_element_type=...  36.7 us
    dot_general x1, other arithmetic, synthesize(): jnp.einsum('stcl,scq->tlq', coeff_rows, high_part, preferred_element_type...  36.1 us
    all_to_all x2, local copies, waits for them, and re-layouts, shards(): lax.all_to_all(grid_local, 'field', split_axis=2, concat_axis=1, tiled=True)  28.6 us
    convert_element_type x1, local copies, waits for them, and re-layouts, synthesize(): return (from_high + from_low).astype(jnp.bfloat16)  19.3 us
    all_to_all x2, local copies, waits for them, and re-layouts, shards(): lax.all_to_all(coeffs, 'wave', split_axis=1, concat_axis=0, tiled=True)  18.7 us
  transfers between devices with their start and end apart: 2, of which 1 were waited for; matrix products, arithmetic and copies ran while one was open for 16% of the time, Pallas kernels for 0%

commit v1 on v0

--- a/solution.py
+++ b/solution.py
@@ -62,7 +62,26 @@
     by_latitude = lax.all_to_all(coeffs, "wave", split_axis=1, concat_axis=0, tiled=True)
     high_part, low_part = fourier_tables(wave_slot, jnp.arange(NLON, dtype=jnp.int32))
     grid_local = synthesize(by_latitude, high_part, low_part)
-    columns = lax.all_to_all(grid_local, "field", split_axis=2, concat_axis=1, tiled=True)
+    val, side_arr = (jax.lax.axis_size("field"), jax.lax.axis_index("field"))
+    part_now = grid_local.shape[2] // val
+    odd = list(grid_local.shape)
+    odd[2] = part_now
+    e_next = odd[1]
+    odd[1] = e_next * val
+    columns = jnp.zeros(odd, grid_local.dtype)
+    src_i = 0
+    while src_i < val:
+        p_next = lax.dynamic_slice_in_dim(
+            grid_local, (side_arr ^ src_i) * part_now, part_now, axis=2
+        )
+        if src_i:
+            p_next = jax.lax.ppermute(
+                p_next, axis_name="field", perm=[(at, at ^ src_i) for at in range(val)]
+            )
+        columns = lax.dynamic_update_slice_in_dim(
+            columns, p_next, (side_arr ^ src_i) * e_next, axis=1
+        )
+        src_i += 1
     return jnp.take(columns, level_order, axis=1)
 
 

time: 458 us -> 328 us (0.72); the launches traced: 450 us -> 326 us
  local copies, waits for them, and re-layouts: 247 us -> 137 us
  waiting for transfers between devices: 56.3 us -> 46.5 us
    unnamed x15 -> x13, local copies, waits for them, and re-layouts: 105 us -> 32.3 us
    all_to_all x1 -> x0, waiting for transfers between devices: 56.3 us -> none  [shards(): lax.all_to_all(grid_local, 'field', split_axis=2, concat_axis=1, tiled=True)]
    ppermute x0 -> x3, waiting for transfers between devices: none -> 46.5 us  [shards(): jax.lax.ppermute(p_next, axis_name='field', perm=[(at, at ^ src_i) for at...]
    all_to_all x2 -> x0, local copies, waits for them, and re-layouts: 28.6 us -> none  [shards(): lax.all_to_all(grid_local, 'field', split_axis=2, concat_axis=1, tiled=True)]
    convert_element_type x1 -> x0, local copies, waits for them, and re-layouts: 19.3 us -> none  [synthesize(): return (from_high + from_low).astype(jnp.bfloat16)]
    dynamic_update_slice x0 -> x4, local copies, waits for them, and re-layouts: none -> 6.79 us  [shards(): lax.dynamic_update_slice_in_dim(columns, p_next, (side_arr ^ src_i) * e_n...]
    all_to_all x1 -> x0, starting transfers between devices: 5.37 us -> none  [shards(): lax.all_to_all(grid_local, 'field', split_axis=2, concat_axis=1, tiled=True)]
  transfers between devices with their start and end apart: 2 -> 4, of which waited for: 1 -> 3; matrix products, arithmetic and copies ran while one was open for 16% -> 25% of each run, Pallas kernels for 0% -> 0%
where the time goes in v1:
time: 328 us; the launch traced here: 326 us
  local copies, waits for them, and re-layouts  137 us (42%)
  other arithmetic  98.1 us (30%)
  waiting for transfers between devices  46.5 us (14%)
  matrix products  27.2 us (8%)
  starting transfers between devices  17 us (5%)
    ppermute x3, waiting for transfers between devices, shards(): jax.lax.ppermute(p_next, axis_name='field', perm=[(at, at ^ src_i) for at...  46.5 us
    gather x1, local copies, waits for them, and re-layouts, shards(): coeffs = jnp.take(coeffs, lat_order, axis=1)  46.4 us
    dot_general x1, other arithmetic, synthesize(): jnp.einsum('stcl,scq->tlq', coeff_rows, low_part, preferred_element_type=...  36.7 us
    dot_general x1, other arithmetic, synthesize(): jnp.einsum('stcl,scq->tlq', coeff_rows, high_part, preferred_element_type...  36.2 us
    unnamed x13, local copies, waits for them, and re-layouts  32.3 us
    all_to_all x2, local copies, waits for them, and re-layouts, shards(): lax.all_to_all(coeffs, 'wave', split_axis=1, concat_axis=0, tiled=True)  18.7 us
    all_to_all x1, starting transfers between devices, shards(): lax.all_to_all(coeffs, 'wave', split_axis=1, concat_axis=0, tiled=True)  13.2 us
    unnamed x1, other arithmetic  11.2 us
  transfers between devices with their start and end apart: 4, of which 3 were waited for; matrix products, arithmetic and copies ran while one was open for 25% of the time, Pallas kernels for 0%

profile of v1, /device:TPU:1, one launch (start us, length us, event | category | flops | bytes accessed | tf_op | source)
XLA Modules:
  0.0 326.4 jit_solution(17147614925112862890)
XLA Ops:
  2.3 12.9 %copy.9 = bf16[10,640,640]{1,2,0:T(8,128)(2,1)} copy(bf16[10,640,640]{2,1,0:T(8,128)(2,1)} %param.7) | data formatting | bytes 16384000 | tf_op args[1]
  16.0 7.6 %bitcast_select_fusion = bf16[10,640,640]{1,2,0:T(8,128)(2,1)} fusion(bf16[10,640,640]{1,2,0:T(8,128)(2,1)} %copy.9, pred[10,640,10]{1,2,0:T(8,128)(4,1)S(1)} %gt.16), kind=kLoop, calls=%fused_computation.3 | loop fusion | flops 4096000 | bytes 16448000 | tf_op jit(solution)/shard_map/jit(_where)/select_n | solution.py:53
  23.6 6.5 %fusion.6 = f32[10,640,2,40]{1,3,2,0:T(8,128)S(1)} fusion(bf16[10,640,640]{1,2,0:T(8,128)(2,1)} %bitcast_select_fusion, bf16[10,2,40,640]{3,2,1,0:T(8,128)(2,1)S(1)} %copy-done.1, pred[10,640]{1,0:T(8,128)(4,1)S(1)} %get-tuple-element.11), kind=kOutput, calls=%fused_computation.15 | convolution fusion | flops 655872000 | bytes 11270400 | tf_op jit(solution)/shard_map/snj,scln->sjcl/dot_general | solution.py:57
  30.1 3.0 fusion.44
  33.4 2.5 rev.3
  37.3 9.8 %copy.12 = bf16[10,1280,2,40]{3,2,1,0:T(2,128)(2,1)} copy(bf16[10,1280,2,40]{1,3,2,0:T(8,128)(2,1)S(1)} %pad_maximum_fusion) | data formatting | bytes 4096000 | tf_op jit(solution)/shard_map/concatenate | solution.py:60
  47.1 46.4 %gather_fusion = bf16[1280,10,2,40]{3,2,1,0:T(2,128)(2,1)} fusion(bf16[10,1280,2,40]{3,2,1,0:T(2,128)(2,1)} %copy.12, s32[2048]{0:T(1024)S(1)} %pad_clamp_fusion), kind=kCustom, calls=%fused_computation | custom fusion | bytes 4101120 | tf_op jit(solution)/shard_map/jit(_take)/gather | solution.py:61
  93.5 11.2 %fusion.45 = bf16[1280,10,2,40]{3,2,1,0:T(2,128)(2,1)} fusion(bf16[1280,10,2,40]{3,2,1,0:T(2,128)(2,1)} %gather_fusion, pred[1280]{0:T(1024)(128)(4,1)S(1)} %compare_and_fusion), kind=kLoop, calls=%fused_computation.73 | loop fusion | flops 1024000 | bytes 4097280
  104.7 11.3 %reshape.183 = bf16[64,2,8000]{2,1,0:T(2,128)(2,1)} reshape(bf16[1280,10,2,40]{3,2,1,0:T(2,128)(2,1)} %fusion.45) | data formatting | bytes 4096000
  116.1 13.2 %all-to-all-start = ((bf16[64,2,8000]{2,1,0:T(2,128)(2,1)}), bf16[64,2,8000]{2,1,0:T(2,128)(2,1)S(1)}, u32[]{:S(2)}, u32[]{:S(2)}) async-start(bf16[64,2,8000]{2,1,0:T(2,128)(2,1)} %reshape.183), calls=%async_computation | async-start | bytes 4128768 | tf_op jit(solution)/shard_map/all_to_all | solution.py:62
  129.3 36.2 %fusion.54 = bf16[640,2,3072,1]{2,0,1,3:T(8,128)(2,1)} fusion(f32[640]{0:T(1024)S(1)} %get-tuple-element.10, s32[640]{0:T(1024)S(1)} %copy-done.3, f32[640]{0:T(1024)S(1)} %get-tuple-element.9, pred[640,2]{0,1:T(4,128)(4,1)S(1)} %fusion.34), kind=kLoop, calls=%fused_computation.22.clone.clone.clone.1 | loop fusion | flops 51118080 | bytes 7873280 | tf_op jit(solution)/shard_map/stcl,scq->tlq/dot_general | solution.py:35
  165.4 36.7 %fusion.56 = bf16[640,2,3072,1]{2,0,1,3:T(8,128)(2,1)} fusion(f32[640]{0:T(1024)S(1)} %get-tuple-element.10, s32[640]{0:T(1024)S(1)} %copy-done.3, f32[640]{0:T(1024)S(1)} %get-tuple-element.9, pred[640,2]{0,1:T(4,128)(4,1)S(1)} %fusion.34), kind=kLoop, calls=%fused_computation.19.clone.clone.1 | loop fusion | flops 62914560 | bytes 7873280 | tf_op jit(solution)/shard_map/stcl,scq->tlq/dot_general | solution.py:38
  202.1 8.0 %reshape.184 = bf16[1280,10,2,40]{3,2,1,0:T(2,128)(2,1)} reshape(bf16[64,2,8000]{2,1,0:T(2,128)(2,1)S(1)} %all-to-all-done) | data formatting | bytes 4096000
  210.2 6.8 %copy.14 = bf16[64,10,20,2,40]{4,3,2,1,0:T(2,128)(2,1)} copy(bf16[64,10,20,2,40]{4,3,1,2,0:T(2,128)(2,1)} %bitcast.57) | data formatting | bytes 4096000 | tf_op jit(solution)/shard_map/all_to_all | solution.py:62
  217.0 11.9 %copy.15 = bf16[640,20,2,40]{0,3,2,1:T(8,128)(2,1)S(1)} copy(bf16[640,20,2,40]{3,2,1,0:T(2,128)(2,1)} %bitcast.58) | data formatting | bytes 4096000 | tf_op jit(solution)/shard_map/all_to_all | solution.py:62
  228.9 8.9 %fusion.11 = f32[20,40,3072,1]{2,1,3,0:T(8,128)S(1)} fusion(bf16[640,20,2,40]{0,3,2,1:T(8,128)(2,1)S(1)} %copy.15, bf16[640,2,3072,1]{2,0,1,3:T(8,128)(2,1)} %fusion.56), kind=kOutput, calls=%fused_computation.20 | convolution fusion | flops 6291456000 | bytes 19742720 | tf_op jit(solution)/shard_map/stcl,scq->tlq/dot_general | solution.py:38
  237.8 8.9 %fusion.5 = bf16[20,40,3072]{2,1,0:T(8,128)(2,1)S(1)} fusion(f32[20,40,3072,1]{2,1,3,0:T(8,128)S(1)} %fusion.11, bf16[640,20,2,40]{0,3,2,1:T(8,128)(2,1)S(1)} %copy.15, bf16[640,2,3072,1]{2,0,1,3:T(8,128)(2,1)} %fusion.54), kind=kOutput, calls=%fused_computation.14 | convolution fusion | flops 6296371200 | bytes 24657920 | tf_op jit(solution)/shard_map/stcl,scq->tlq/dot_general | solution.py:35
  252.5 2.9 broadcast_in_dim.82
  256.8 20.0 %collective-permute-done = bf16[20,40,768]{2,1,0:T(8,128)(2,1)} collective-permute-done((bf16[20,40,768]{2,1,0:T(8,128)(2,1)}, bf16[20,40,768]{2,1,0:T(8,128)(2,1)}, u32[]{:S(2)}, u32[]{:S(2)}) %collective-permute-start) | collective-permute-done | bytes 1228832 | tf_op jit(solution)/shard_map/ppermute | solution.py:78
  276.9 2.7 copy_dynamic-update-slice_fusion.2
  279.5 25.8 %collective-permute-done.1 = bf16[20,40,768]{2,1,0:T(8,128)(2,1)S(1)} collective-permute-done((bf16[20,40,768]{2,1,0:T(8,128)(2,1)}, bf16[20,40,768]{2,1,0:T(8,128)(2,1)S(1)}, u32[]{:S(2)}, u32[]{:S(2)}) %collective-permute-start.1) | collective-permute-done | bytes 1228832 | tf_op jit(solution)/shard_map/ppermute | solution.py:78
  308.8 11.1 %gather_fusion.1 = bf16[160,20,768]{2,1,0:T(8,128)(2,1)} fusion(bf16[20,160,768]{2,0,1:T(8,128)(2,1)} %copy_dynamic-update-slice_fusion, s32[1024]{0:T(1024)S(1)} %pad_clamp_fusion.1), kind=kCustom, calls=%fused_computation.1 | custom fusion | bytes 9831040 | tf_op jit(solution)/shard_map/jit(_take)/gather | solution.py:85
  319.8 3.3 %select_bitcast_fusion = bf16[20,160,768]{2,0,1:T(8,128)(2,1)S(1)} fusion(bf16[160,20,768]{2,1,0:T(8,128)(2,1)} %gather_fusion.1, pred[160]{0:T(512)(128)(4,1)S(1)} %compare_and_fusion.1), kind=kLoop, calls=%fused_computation.25 | loop fusion | flops 2457600 | bytes 9830560 | tf_op jit(solution)/shard_map/jit(_take)/select_n | solution.py:85
  323.1 3.3 %copy.21 = bf16[20,160,768]{2,1,0:T(8,128)(2,1)} copy(bf16[20,160,768]{2,0,1:T(8,128)(2,1)S(1)} %select_bitcast_fusion) | data formatting | bytes 9830400 | tf_op jit(solution)/shard_map/jit(_take)/select_n | solution.py:85
  (35 shorter events, 15.4 us)
Async XLA Ops:
  2.3 12.9 %copy-start.2 = (s32[10,10,10]{2,1,0:T(8,128)S(1)}, s32[10,10,10]{2,1,0:T(8,128)}, u32[]{:S(2)}) copy-start(s32[10,10,10]{2,1,0:T(8,128)} %param.8) | copy-start | bytes 12004
  16.0 7.6 %copy-start.1 = (bf16[10,2,40,640]{3,2,1,0:T(8,128)(2,1)S(1)}, bf16[10,2,40,640]{3,2,1,0:T(8,128)(2,1)}, u32[]{:S(2)}) copy-start(bf16[10,2,40,640]{3,2,1,0:T(8,128)(2,1)} %param.6) | copy-start | bytes 3072004
  23.6 6.5 %copy-start = (bf16[10,640,640]{1,2,0:T(8,128)(2,1)S(1)}, bf16[10,640,640]{1,2,0:T(8,128)(2,1)}, u32[]{:S(2)}) copy-start(bf16[10,640,640]{1,2,0:T(8,128)(2,1)} %bitcast_select_fusion) | copy-start | bytes 24576004
  104.7 24.6 %copy-start.3 = (s32[640]{0:T(1024)S(1)}, s32[640]{0:T(1024)}, u32[]{:S(2)}) copy-start(s32[640]{0:T(1024)} %param.9) | copy-start | bytes 7684
  116.1 86.1 %all-to-all-start = ((bf16[64,2,8000]{2,1,0:T(2,128)(2,1)}), bf16[64,2,8000]{2,1,0:T(2,128)(2,1)S(1)}, u32[]{:S(2)}, u32[]{:S(2)}) async-start(bf16[64,2,8000]{2,1,0:T(2,128)(2,1)} %reshape.183), calls=%async_computation | async-start | bytes 4128768 | tf_op jit(solution)/shard_map/all_to_all | solution.py:62
  246.6 5.7 %copy-start.4 = (s32[160]{0:T(256)S(1)}, s32[160]{0:T(256)}, u32[]{:S(2)}) copy-start(s32[160]{0:T(256)} %param.11) | copy-start | bytes 1924
  248.7 28.2 %collective-permute-start = (bf16[20,40,768]{2,1,0:T(8,128)(2,1)}, bf16[20,40,768]{2,1,0:T(8,128)(2,1)}, u32[]{:S(2)}, u32[]{:S(2)}) collective-permute-start(bf16[20,40,768]{2,1,0:T(8,128)(2,1)} %get-tuple-element.7), channel_id=1, source_target_pairs={{0,1},{1,0},{2,3},{3,2},{4,5},{5,4},{6,7},{7,6},{8,9},{9,8},{10,11... | collective-permute-start | bytes 3686408 | tf_op jit(solution)/shard_map/ppermute | solution.py:78
  249.9 55.5 %collective-permute-start.1 = (bf16[20,40,768]{2,1,0:T(8,128)(2,1)}, bf16[20,40,768]{2,1,0:T(8,128)(2,1)S(1)}, u32[]{:S(2)}, u32[]{:S(2)}) collective-permute-start(bf16[20,40,768]{2,1,0:T(8,128)(2,1)} %get-tuple-element.6), channel_id=1, source_target_pairs={{0,2},{1,3},{2,0},{3,1},{4,6},{5,7},{6,4},{7,5},{8,10},{9,11},{10,... | collective-permute-start | bytes 3686408 | tf_op jit(solution)/shard_map/ppermute | solution.py:78
  252.3 55.0 %collective-permute-start.2 = (bf16[20,40,768]{2,1,0:T(8,128)(2,1)}, bf16[20,40,768]{2,1,0:T(8,128)(2,1)S(1)}, u32[]{:S(2)}, u32[]{:S(2)}) collective-permute-start(bf16[20,40,768]{2,1,0:T(8,128)(2,1)} %get-tuple-element.5), channel_id=1, source_target_pairs={{0,3},{1,2},{2,1},{3,0},{4,7},{5,6},{6,5},{7,4},{8,11},{9,10},{10,... | collective-permute-start | bytes 3686408 | tf_op jit(solution)/shard_map/ppermute | solution.py:78
